TPU v7x, 256 devices: a whole 4x4x8 slice. The times are simulated.
256 devices in a mesh: mode: 16 (over x_hi, y, core), site: 16 (over z, x_lo).
Axes of the slice: x: 4 (x_hi: 2, x_lo: 2; x = x_hi * 2 + x_lo), y: 4, z: 8, core: 2. Of those that a mesh axis runs over, the one named last changes fastest.
Arguments:
- eigvecs: bfloat16 [2, 64, 3, 110592], P(None, 'mode', None, 'site'), may hold values from -6 to 6
- perams: bfloat16 [2, 16, 64, 64], replicated, may hold values from -0.75 to 0.75
- momenta: int32 [2, 3], replicated, may hold values from -2 to 2
- spins: int32 [16, 3], replicated, may hold values from 0 to 15
- pair_combs: int32 [16, 2], P('site'), may hold values from 0 to 15
- pair_moms: int32 [16, 2], P('site'), may hold values from 0 to 1
Outputs:
- exchange: float32 [16, 2, 64, 64], P('site', None, 'mode')
All inputs are finite; a program needn't handle non-finite values.
Results may differ from a plain program's by a relative error of at most 0.018.
Values may be sent and summed in bfloat16 or wider, within the bound.
No kernel may reach another device: no remote copies, remote signals or barrier semaphores. Data moves between devices by JAX's collectives and lax.ppermute only.
A program may use at most 64 MiB of HBM per device.

v0:
```python
import jax
import jax.numpy as jnp
from jax import lax
from jax.sharding import PartitionSpec as P

LAT = 48


def hartley(momenta, glob):
    coord_x = glob // (LAT * LAT)
    coord_y = glob // LAT % LAT
    coord_z = glob % LAT
    wave = (
        momenta[:, 0:1] * coord_x[None]
        + momenta[:, 1:2] * coord_y[None]
        + momenta[:, 2:3] * coord_z[None]
    ) % LAT
    theta = wave.astype(jnp.float32) * (2.0 * jnp.pi / LAT)
    return jnp.cos(theta) + jnp.sin(theta)


def body(eigvecs, perams, momenta, spins, pair_combs, pair_moms):
    nslice, mode_dev, _, site_dev = eigvecs.shape
    nmode = perams.shape[-1]
    nspin = perams.shape[1]
    ncomb = spins.shape[0]
    nmom = momenta.shape[0]
    comb_dev = ncomb // lax.axis_size("site")
    first_mode = lax.axis_index("mode") * mode_dev
    gathered = lax.all_gather(eigvecs, "mode", axis=1, tiled=True)
    glob = lax.axis_index("site") * site_dev + jnp.arange(site_dev, dtype=jnp.int32)
    phase = hartley(momenta, glob)

    def triplet_part(vectors):
        floats = vectors.astype(jnp.float32)
        own_modes = lax.dynamic_slice_in_dim(floats, first_mode, mode_dev, 0)
        left = own_modes[:, None]
        right = floats[None]
        cross_0 = left[:, :, 1] * right[:, :, 2] - left[:, :, 2] * right[:, :, 1]
        cross_1 = left[:, :, 2] * right[:, :, 0] - left[:, :, 0] * right[:, :, 2]
        cross_2 = left[:, :, 0] * right[:, :, 1] - left[:, :, 1] * right[:, :, 0]
        diquark = jnp.stack([cross_0, cross_1, cross_2], axis=2).astype(jnp.bfloat16)
        weighted = (phase[:, None, None, :] * floats[None]).astype(jnp.bfloat16)
        product = lax.dot_general(
            diquark.reshape(mode_dev * nmode, 3 * site_dev),
            weighted.reshape(nmom * nmode, 3 * site_dev),
            (((1,), (1,)), ((), ())),
            preferred_element_type=jnp.float32,
        )
        return product.reshape(mode_dev, nmode, nmom, nmode)

    partial_sums = lax.map(triplet_part, gathered)
    totals = lax.psum(partial_sums, "site")
    triplet = (totals * float(LAT) ** (-1.5)).astype(jnp.bfloat16)
    comb_ids = jnp.arange(ncomb, dtype=jnp.int32)
    mom_ids = jnp.arange(nmom, dtype=jnp.int32)
    spin_ids = jnp.arange(nspin, dtype=jnp.int32)
    own_spins = lax.dynamic_slice_in_dim(spins, lax.axis_index("site") * comb_dev, comb_dev, 0)
    picker = (own_spins[:, :, None] == spin_ids[None, None, :]).astype(jnp.bfloat16)
    chosen = jnp.einsum(
        "cks,tsmn->tckmn", picker, perams, preferred_element_type=jnp.float32
    ).astype(jnp.bfloat16)
    first = jnp.einsum(
        "tijpk,tcmk->tcijpm", triplet, chosen[:, :, 2], preferred_element_type=jnp.float32
    ).astype(jnp.bfloat16)
    second = jnp.einsum(
        "tcmj,tcijpk->itcpmk", chosen[:, :, 1], first, preferred_element_type=jnp.float32
    ).astype(jnp.bfloat16)
    rows_sel = chosen[:, :, 0]
    cols_sel = lax.dynamic_slice_in_dim(rows_sel, first_mode, mode_dev, 3)
    own_blocks = lax.psum_scatter(
        jnp.einsum("tcmi,itcpjk->mtcpjk", cols_sel, second, preferred_element_type=jnp.float32),
        "mode",
        scatter_dimension=0,
        tiled=True,
    ).astype(jnp.bfloat16)
    all_blocks = lax.all_gather(own_blocks, "site", axis=2, tiled=True)
    swapped = lax.all_to_all(all_blocks, "mode", split_axis=4, concat_axis=0, tiled=True)
    pick_left = (
        (pair_combs[:, 0][:, None, None] == comb_ids[None, :, None])
        & (pair_moms[:, 0][:, None, None] == mom_ids[None, None, :])
    ).astype(jnp.bfloat16)
    pick_right = (
        (pair_combs[:, 1][:, None, None] == comb_ids[None, :, None])
        & (pair_moms[:, 1][:, None, None] == mom_ids[None, None, :])
    ).astype(jnp.bfloat16)
    left_block = jnp.einsum(
        "qcp,itcpjk->qtijk", pick_left, all_blocks, preferred_element_type=jnp.float32
    ).astype(jnp.bfloat16)
    right_block = jnp.einsum(
        "qcp,mtcpnk->qtmnk", pick_right, swapped, preferred_element_type=jnp.float32
    ).astype(jnp.bfloat16)
    partial_corr = jnp.einsum(
        "qtijk,qtjil->qtkl", left_block, right_block, preferred_element_type=jnp.float32
    ) * (1.0 / nmode)
    return lax.psum_scatter(
        partial_corr.astype(jnp.bfloat16), "mode", scatter_dimension=2, tiled=True
    ).astype(jnp.float32)


def solution(mesh):
    placed = (P(None, "mode", None, "site"), P(), P(), P(), P("site", None), P("site", None))
    return jax.shard_map(
        body, mesh=mesh, in_specs=placed, out_specs=P("site", None, "mode", None), check_vma=False
    )
```

profile of v0, /device:TPU:38, one launch (start us, length us, event | category | flops | bytes accessed | tf_op | source)
XLA Modules:
  0.0 601.7 jit_solution(13482562929319963017)
XLA Ops:
  6.5 2.0 copy.22
  8.7 0.9 dynamic-slice_reduce_fusion
  9.5 1.0 slice_reduce_fusion
  11.1 64.4 %all-gather.3.cloned.1.call-done = bf16[2,64,3,6912]{3,0,2,1:T(2,128)(2,1)} async-done(((bf16[2,4,3,6912]{3,0,2,1:T(2,128)(2,1)}), bf16[2,64,3,6912]{3,0,2,1:T(2,128)(2,1)}) %all-gather.3.cloned.1.call-update) | async-done | bytes 5308432 | tf_op jit(solution)/shard_map/all_gather | solution.py:30
  75.5 5.4 copy.23
  80.9 20.2 %while.13 = (s32[]{:T(128)}, f32[2,4,64,2,64]{4,2,3,1,0:T(8,128)S(1)}, bf16[2,64,3,6912]{3,1,2,0:T(8,128)(2,1)}, s32[]{:T(128)}, s32[6912]{0:T(1024)S(1)}, /*ind...) while((s32[]{:T(128)}, ...), condition=%wide.region_1.2_spmd.clone, body=%wide.region_0.1_spmd.clone.sunk | while | flops 1418867712 | bytes 57853072 | solution.py:52
  80.9 2.4 dynamic-slice_convert_fusion.3
  83.8 3.2 subtract_convert_fusion.4
  86.9 1.0 sine_add_fusion.2
  88.0 3.0 fusion.62
  91.0 2.4 dynamic-slice_convert_fusion.3
  93.9 3.2 subtract_convert_fusion.4
  97.0 1.0 sine_add_fusion.2
  98.1 3.0 fusion.62
  101.1 0.8 copy-done.2
  102.3 135.7 %all-reduce.3.cloned.1.call-done = f32[2,4,64,2,64]{4,2,3,1,0:T(8,128)} async-done(((f32[2,4,64,2,64]{4,2,3,1,0:T(8,128)}), f32[2,4,64,2,64]{4,2,3,1,0:T(8,128)}) %all-reduce.3.cloned.1.call-update) | async-done | bytes 262160 | tf_op jit(solution)/shard_map/psum | solution.py:53
  238.1 1.6 fusion.22
  239.8 4.9 convolution_bitcast_fusion
  244.8 9.1 %copy.26 = f32[64,2,1,2,64,64]{5,4,3,2,1,0:T(8,128)} copy(f32[64,2,1,2,64,64]{0,5,4,3,1,2:T(8,128)} %convolution_bitcast_fusion) | data formatting | bytes 8388608 | tf_op jit(solution)/shard_map/tcmi,itcpjk->mtcpjk/transpose | solution.py:72
  254.1 109.6 %reduce-scatter.3.cloned.1.call-done = f32[4,2,1,2,64,64]{5,4,3,2,1,0:T(8,128)} async-done(((f32[64,2,1,2,64,64]{5,4,3,2,1,0:T(8,128)}), f32[4,2,1,2,64,64]{5,4,3,2,1,0:T(8,128)}) %reduce-scatter.3.cloned.1.call-update) | async-done | bytes 262160 | tf_op jit(solution)/shard_map/reduce_scatter | solution.py:71
  363.7 1.8 convert_bitcast_fusion
  365.5 99.9 %all-gather.5.cloned.1.call-done = bf16[4,2,16,2,64,64]{5,4,3,1,0,2:T(8,128)(2,1)} async-done(((bf16[4,2,1,2,64,64]{5,4,3,1,0,2:T(8,128)(2,1)}), bf16[4,2,16,2,64,64]{5,4,3,1,0,2:T(8,128)(2,1)}) %all-gather.5.cloned.1.call-update) | async-done | bytes 2097168 | tf_op jit(solution)/shard_map/all_gather | solution.py:77
  465.4 6.9 %copy.74 = bf16[4,2,16,2,64,64]{5,2,3,1,0,4:T(8,128)(2,1)} copy(bf16[4,2,16,2,64,64]{5,4,3,1,0,2:T(8,128)(2,1)} %all-gather.5.cloned.1.call-done) | data formatting | bytes 4194304 | tf_op jit(solution)/shard_map/all_gather | solution.py:77
  472.3 7.6 %reshape.298 = bf16[16,2,32768]{2,1,0:T(2,128)(2,1)} reshape(bf16[64,4,2,2,16,64]{5,4,3,2,1,0:T(8,128)(2,1)} %bitcast.161) | data formatting | bytes 4194304
  479.9 7.3 %all-to-all-start = ((bf16[16,2,32768]{2,1,0:T(2,128)(2,1)}), bf16[16,2,32768]{2,1,0:T(2,128)(2,1)S(1)}, u32[]{:S(2)}, u32[]{:S(2)}) async-start(bf16[16,2,32768]{2,1,0:T(2,128)(2,1)} %reshape.298), calls=%async_computation.1 | async-start | bytes 4194304 | tf_op jit(solution)/shard_map/all_to_all | solution.py:78
  491.5 0.7 iota_compare_fusion.4
  492.3 3.4 multiply_reduce_fusion
  495.8 18.6 %all-to-all-done = bf16[16,2,32768]{2,1,0:T(2,128)(2,1)S(1)} async-done(((bf16[16,2,32768]{2,1,0:T(2,128)(2,1)}), bf16[16,2,32768]{2,1,0:T(2,128)(2,1)S(1)}, u32[]{:S(2)}, u32[]{:S(2)}) %all-to-all-start) | async-done | bytes 2097184 | tf_op jit(solution)/shard_map/all_to_all | solution.py:78
  514.4 5.0 reshape.299
  519.4 3.4 copy.30
  522.8 0.7 convolution_bitcast_fusion.1
  523.8 70.8 %all-reduce = bf16[1,2,64,64]{3,2,1,0:T(8,128)(2,1)S(1)} all-reduce(bf16[1,2,64,64]{3,2,1,0:T(8,128)(2,1)S(1)} %fusion.26), channel_id=3, replica_groups=mesh['mode'=16,'site'=16] {'mode'}, use_global_device_ids=true, to_apply=%region_4.5.clone | all-reduce | flops 8192 | bytes 32768
  (44 shorter events, 7.1 us)
Async XLA Ops:
  6.5 4.1 copy-start
  6.5 68.9 %all-gather.3.cloned.1.call-start = ((), (), s32[]{:S(2)}) async-start(), calls=%async_computation.2 | async-start | bytes 5640192 | tf_op jit(solution)/shard_map/all_gather | solution.py:30
  8.6 229.5 %all-reduce.3.cloned.1.call-start = ((), (), s32[]{:S(2)}) async-start(), calls=%async_computation.3 | async-start | bytes 1048576 | tf_op jit(solution)/shard_map/psum | solution.py:53
  101.1 0.8 copy-start.2
  101.9 261.8 %reduce-scatter.3.cloned.1.call-start = ((), (), s32[]{:S(2)}) async-start(), calls=%async_computation.4 | async-start | bytes 8912896 | tf_op jit(solution)/shard_map/reduce_scatter | solution.py:71
  253.9 211.5 %all-gather.5.cloned.1.call-start = ((), (), s32[]{:S(2)}) async-start(), calls=%async_computation.5 | async-start | bytes 4456448 | tf_op jit(solution)/shard_map/all_gather | solution.py:77
  472.3 14.9 %copy-start.5 = (u32[256]{0:T(256)S(1)}, u32[256]{0:T(256)}, u32[]{:S(2)}) copy-start(u32[256]{0:T(256)} %constant.88) | copy-start | bytes 3076
  472.3 16.1 %copy-start.3 = (s32[1,2]{1,0:T(1,128)S(1)}, s32[1,2]{1,0:T(1,128)}, u32[]{:S(2)}) copy-start(s32[1,2]{1,0:T(1,128)} %param.13) | copy-start | bytes 28
  472.3 17.3 %copy-start.4 = (s32[1,2]{1,0:T(1,128)S(1)}, s32[1,2]{1,0:T(1,128)}, u32[]{:S(2)}) copy-start(s32[1,2]{1,0:T(1,128)} %param.12) | copy-start | bytes 28
  479.9 34.5 %all-to-all-start = ((bf16[16,2,32768]{2,1,0:T(2,128)(2,1)}), bf16[16,2,32768]{2,1,0:T(2,128)(2,1)S(1)}, u32[]{:S(2)}, u32[]{:S(2)}) async-start(bf16[16,2,32768]{2,1,0:T(2,128)(2,1)} %reshape.298), calls=%async_computation.1 | async-start | bytes 4194304 | tf_op jit(solution)/shard_map/all_to_all | solution.py:78
  519.4 75.7 %copy-start.1 = (bf16[2,16,64,64]{3,2,1,0:T(8,128)(2,1)S(1)}, bf16[2,16,64,64]{3,2,1,0:T(8,128)(2,1)}, u32[]{:S(2)}) copy-start(bf16[2,16,64,64]{3,2,1,0:T(8,128)(2,1)} %param.9) | copy-start | bytes 786436
Sparse Core Ops, SparseCore 0:
  10.0 65.4 all-gather.2
  102.0 136.0 all-reduce.2
  254.0 109.6 reduce-scatter.2
  365.6 99.7 all-gather.4
where the time goes:
time: 602 us
  waiting for transfers between devices  428 us (71%)
  blocking collectives  70.8 us (12%)
  local copies, waits for them, and re-layouts  45.4 us (8%)
  other arithmetic  21.7 us (4%)
  between operations  13.9 us (2%)
  matrix products  13.8 us (2%)
  starting transfers between devices  7.58 us (1%)
    psum x1, waiting for transfers between devices, body(): totals = lax.psum(partial_sums, 'site')  136 us
    reduce_scatter x1, waiting for transfers between devices, body(): lax.psum_scatter(jnp.einsum('tcmi,itcpjk->mtcpjk', cols_sel, second, pref...  110 us
    all_gather x1, waiting for transfers between devices, body(): all_blocks = lax.all_gather(own_blocks, 'site', axis=2, tiled=True)  99.9 us
    unnamed x1, blocking collectives  70.8 us
    all_gather x1, waiting for transfers between devices, body(): gathered = lax.all_gather(eigvecs, 'mode', axis=1, tiled=True)  64.4 us
    unnamed x17, local copies, waits for them, and re-layouts  21.4 us
    all_to_all x1, waiting for transfers between devices, body(): lax.all_to_all(all_blocks, 'mode', split_axis=4, concat_axis=0, tiled=True)  18.6 us
  transfers between devices with their start and end apart: 5, of which 5 were waited for; matrix products, arithmetic and copies ran while one was open for 2% of the time, Pallas kernels for 0%

commit v1 on v0

--- a/solution.py
+++ b/solution.py
@@ -74,7 +74,9 @@
         scatter_dimension=0,
         tiled=True,
     ).astype(jnp.bfloat16)
-    all_blocks = lax.all_gather(own_blocks, "site", axis=2, tiled=True)
+    all_blocks = jnp.concatenate(
+        lax.all_to_all(jnp.stack([own_blocks] * lax.axis_size("site")), "site", 0, 0), axis=2
+    )
     swapped = lax.all_to_all(all_blocks, "mode", split_axis=4, concat_axis=0, tiled=True)
     pick_left = (
         (pair_combs[:, 0][:, None, None] == comb_ids[None, :, None])

time: 602 us -> 577 us (0.958)
  waiting for transfers between devices: 428 us -> 327 us
  blocking collectives: 70.8 us -> 126 us
  local copies, waits for them, and re-layouts: 45.4 us -> 64.9 us
    all_gather x1 -> x0, waiting for transfers between devices: 99.9 us -> none  [body(): all_blocks = lax.all_gather(own_blocks, 'site', axis=2, tiled=True)]
    all_to_all x0 -> x1, blocking collectives: none -> 55 us  [body(): lax.all_to_all(jnp.stack([own_blocks] * lax.axis_size('site')), 'site', 0...]
    unnamed x17 -> x22, local copies, waits for them, and re-layouts: 21.4 us -> 40 us
    reshape x0 -> x2, local copies, waits for them, and re-layouts: none -> 7.83 us  [body(): jnp.concatenate(lax.all_to_all(jnp.stack([own_blocks] * lax.axis_size('si...]
    all_gather x1 -> x0, local copies, waits for them, and re-layouts: 6.86 us -> none  [body(): all_blocks = lax.all_gather(own_blocks, 'site', axis=2, tiled=True)]
  transfers between devices with their start and end apart: 5 -> 4, of which waited for: 5 -> 4; matrix products, arithmetic and copies ran while one was open for 2% -> 2% of each run, Pallas kernels for 0% -> 0%
where the time goes in v1:
time: 577 us; the launch traced here: 575 us
  waiting for transfers between devices  327 us (57%)
  blocking collectives  126 us (22%)
  local copies, waits for them, and re-layouts  64.9 us (11%)
  matrix products  18.5 us (3%)
  other arithmetic  17.7 us (3%)
  between operations  13.9 us (2%)
  starting transfers between devices  6.72 us (1%)
    psum x1, waiting for transfers between devices, body(): totals = lax.psum(partial_sums, 'site')  136 us
    reduce_scatter x1, waiting for transfers between devices, body(): lax.psum_scatter(jnp.einsum('tcmi,itcpjk->mtcpjk', cols_sel, second, pref...  110 us
    unnamed x1, blocking collectives  70.8 us
    all_gather x1, waiting for transfers between devices, body(): gathered = lax.all_gather(eigvecs, 'mode', axis=1, tiled=True)  64.4 us
    all_to_all x1, blocking collectives, body(): lax.all_to_all(jnp.stack([own_blocks] * lax.axis_size('site')), 'site', 0...  55 us
    unnamed x22, local copies, waits for them, and re-layouts  40 us
    all_to_all x1, waiting for transfers between devices, body(): lax.all_to_all(all_blocks, 'mode', split_axis=4, concat_axis=0, tiled=True)  17.3 us
  transfers between devices with their start and end apart: 4, of which 4 were waited for; matrix products, arithmetic and copies ran while one was open for 2% of the time, Pallas kernels for 0%

profile of v1, /device:TPU:38, one launch (start us, length us, event | category | flops | bytes accessed | tf_op | source)
XLA Modules:
  0.0 574.8 jit_solution(16845803131576096457)
XLA Ops:
  6.5 2.0 copy.20
  11.0 64.4 %all-gather.2.cloned.1.call-done = bf16[2,64,3,6912]{3,0,2,1:T(2,128)(2,1)} async-done(((bf16[2,4,3,6912]{3,0,2,1:T(2,128)(2,1)}), bf16[2,64,3,6912]{3,0,2,1:T(2,128)(2,1)}) %all-gather.2.cloned.1.call-update) | async-done | bytes 5308432 | tf_op jit(solution)/shard_map/all_gather | solution.py:30
  75.5 5.4 copy.21
  80.9 20.2 %while.13 = (s32[]{:T(128)}, f32[2,4,64,2,64]{4,2,3,1,0:T(8,128)S(1)}, bf16[2,64,3,6912]{3,1,2,0:T(8,128)(2,1)}, s32[]{:T(128)}, s32[6912]{0:T(1024)S(1)}, /*ind...) while((s32[]{:T(128)}, ...), condition=%wide.region_1.2_spmd.clone, body=%wide.region_0.1_spmd.clone.sunk | while | flops 1418867712 | bytes 57853072 | solution.py:52
  80.9 2.4 dynamic-slice_convert_fusion.3
  83.8 3.2 subtract_convert_fusion.4
  86.9 1.0 sine_add_fusion.2
  88.0 3.0 fusion.65
  91.0 2.4 dynamic-slice_convert_fusion.3
  93.9 3.2 subtract_convert_fusion.4
  97.0 1.0 sine_add_fusion.2
  98.1 3.0 fusion.65
  102.3 135.5 %all-reduce.3.cloned.1.call-done = f32[2,4,64,2,64]{4,2,3,1,0:T(8,128)} async-done(((f32[2,4,64,2,64]{4,2,3,1,0:T(8,128)}), f32[2,4,64,2,64]{4,2,3,1,0:T(8,128)}) %all-reduce.3.cloned.1.call-update) | async-done | bytes 262160 | tf_op jit(solution)/shard_map/psum | solution.py:53
  237.8 1.6 fusion.24
  239.6 4.9 convolution_bitcast_fusion
  244.6 9.1 %copy.24 = f32[64,2,1,2,64,64]{5,4,3,2,1,0:T(8,128)} copy(f32[64,2,1,2,64,64]{0,5,4,3,1,2:T(8,128)} %convolution_bitcast_fusion) | data formatting | bytes 8388608 | tf_op jit(solution)/shard_map/tcmi,itcpjk->mtcpjk/transpose | solution.py:72
  253.7 109.8 %reduce-scatter.3.cloned.1.call-done = f32[4,2,1,2,64,64]{5,4,3,2,1,0:T(8,128)} async-done(((f32[64,2,1,2,64,64]{5,4,3,2,1,0:T(8,128)}), f32[4,2,1,2,64,64]{5,4,3,2,1,0:T(8,128)}) %reduce-scatter.3.cloned.1.call-update) | async-done | bytes 262160 | tf_op jit(solution)/shard_map/reduce_scatter | solution.py:71
  363.5 1.1 convert_bitcast_fusion
  364.5 3.0 broadcast_bitcast_fusion
  367.5 6.3 %reshape.352 = bf16[16,2,32768]{2,1,0:T(2,128)(2,1)S(1)} reshape(bf16[16,1,4,2,2,64,64]{6,5,4,3,2,1,0:T(8,128)(2,1)} %broadcast_bitcast_fusion) | data formatting | bytes 4194304
  373.9 55.0 %all_to_all.23 = bf16[16,2,32768]{2,1,0:T(2,128)(2,1)} all-to-all(bf16[16,2,32768]{2,1,0:T(2,128)(2,1)S(1)} %reshape.352), channel_id=1, replica_groups=mesh['mode'=16,'site'=16] {'site'}, dimensions={0} | all-to-all | bytes 4194304 | tf_op jit(solution)/shard_map/all_to_all | solution.py:78
  428.9 7.4 %reshape.353 = bf16[16,1,4,2,2,64,64]{6,5,4,3,2,1,0:T(8,128)(2,1)} reshape(bf16[16,2,32768]{2,1,0:T(2,128)(2,1)} %all_to_all.23) | data formatting | bytes 4194304
  436.3 3.1 bitcast_bitcast_fusion
  439.5 1.9 copy-done.2
  441.4 4.7 copy.70
  446.1 7.6 %reshape.354 = bf16[16,2,32768]{2,1,0:T(2,128)(2,1)} reshape(bf16[64,4,2,2,16,64]{5,4,3,2,1,0:T(8,128)(2,1)} %bitcast.176) | data formatting | bytes 4194304
  453.6 6.6 %all-to-all-start.1 = ((bf16[16,2,32768]{2,1,0:T(2,128)(2,1)}), bf16[16,2,32768]{2,1,0:T(2,128)(2,1)S(1)}, u32[]{:S(2)}, u32[]{:S(2)}) async-start(bf16[16,2,32768]{2,1,0:T(2,128)(2,1)} %reshape.354), calls=%async_computation.2 | async-start | bytes 4194304 | tf_op jit(solution)/shard_map/all_to_all | solution.py:80
  465.4 4.6 fusion.21
  470.2 17.3 %all-to-all-done.1 = bf16[16,2,32768]{2,1,0:T(2,128)(2,1)S(1)} async-done(((bf16[16,2,32768]{2,1,0:T(2,128)(2,1)}), bf16[16,2,32768]{2,1,0:T(2,128)(2,1)S(1)}, u32[]{:S(2)}, u32[]{:S(2)}) %all-to-all-start.1) | async-done | bytes 2097184 | tf_op jit(solution)/shard_map/all_to_all | solution.py:80
  487.5 5.0 reshape.355
  492.5 3.4 copy.27
  496.9 70.8 %all-reduce = bf16[1,2,64,64]{3,2,1,0:T(8,128)(2,1)S(1)} all-reduce(bf16[1,2,64,64]{3,2,1,0:T(8,128)(2,1)S(1)} %fusion.28), channel_id=3, replica_groups=mesh['mode'=16,'site'=16] {'mode'}, use_global_device_ids=true, to_apply=%region_4.5.clone | all-reduce | flops 8192 | bytes 32768
  (48 shorter events, 10.9 us)
Async XLA Ops:
  6.5 4.1 copy-start
  6.5 68.9 %all-gather.2.cloned.1.call-start = ((), (), s32[]{:S(2)}) async-start(), calls=%async_computation.3 | async-start | bytes 5640192 | tf_op jit(solution)/shard_map/all_gather | solution.py:30
  8.6 229.3 %all-reduce.3.cloned.1.call-start = ((), (), s32[]{:S(2)}) async-start(), calls=%async_computation.4 | async-start | bytes 1048576 | tf_op jit(solution)/shard_map/psum | solution.py:53
  101.1 0.8 copy-start.3
  101.9 261.6 %reduce-scatter.3.cloned.1.call-start = ((), (), s32[]{:S(2)}) async-start(), calls=%async_computation.5 | async-start | bytes 8912896 | tf_op jit(solution)/shard_map/reduce_scatter | solution.py:71
  439.4 1.9 copy-start.2
  446.1 14.2 %copy-start.6 = (u32[256]{0:T(256)S(1)}, u32[256]{0:T(256)}, u32[]{:S(2)}) copy-start(u32[256]{0:T(256)} %constant.87) | copy-start | bytes 3076
  446.1 15.4 %copy-start.4 = (s32[1,2]{1,0:T(1,128)S(1)}, s32[1,2]{1,0:T(1,128)}, u32[]{:S(2)}) copy-start(s32[1,2]{1,0:T(1,128)} %param.13) | copy-start | bytes 28
  446.1 16.7 %copy-start.5 = (s32[1,2]{1,0:T(1,128)S(1)}, s32[1,2]{1,0:T(1,128)}, u32[]{:S(2)}) copy-start(s32[1,2]{1,0:T(1,128)} %param.12) | copy-start | bytes 28
  453.6 33.9 %all-to-all-start.1 = ((bf16[16,2,32768]{2,1,0:T(2,128)(2,1)}), bf16[16,2,32768]{2,1,0:T(2,128)(2,1)S(1)}, u32[]{:S(2)}, u32[]{:S(2)}) async-start(bf16[16,2,32768]{2,1,0:T(2,128)(2,1)} %reshape.354), calls=%async_computation.2 | async-start | bytes 4194304 | tf_op jit(solution)/shard_map/all_to_all | solution.py:80
  492.5 75.7 %copy-start.1 = (bf16[2,16,64,64]{3,2,1,0:T(8,128)(2,1)S(1)}, bf16[2,16,64,64]{3,2,1,0:T(8,128)(2,1)}, u32[]{:S(2)}) copy-start(bf16[2,16,64,64]{3,2,1,0:T(8,128)(2,1)} %param.9) | copy-start | bytes 786436
Sparse Core Ops, SparseCore 0:
  10.0 65.4 all-gather.1
  102.0 135.8 all-reduce.2
  253.8 109.6 reduce-scatter.2
